TPU v7x, 512 devices: a whole 4x8x8 slice. The times are simulated.
512 devices in a mesh: trans: 64 (over x, z, core), bin: 8 (over y).
Axes of the slice: x: 4, y: 8, z: 8, core: 2. Of those that a mesh axis runs over, the one named last changes fastest.
Arguments:
- pair_density: bfloat16 [32768, 8000], P('trans', 'bin'), may hold values from -1.5 to 1.5
- bin_index: int32 [32768, 1], P('trans'), may hold values from 0 to 255; in each aligned block of 512 rows (0 to 511, 512 to 1023, ...) at most 4 rows name the same one
- panel_columns: int32 [128], replicated, may hold values from 0 to 7999
Outputs:
- response: float32 [2, 256, 1024000], P(None, None, ('bin', 'trans'))
Inputs may be any that keep to these rules, and one draw needn't show every extreme that they name: `bin_index`: among the 512 transitions of one device no bin occurs more than 4 times, and some bin occurs exactly 4 times. `panel_columns`: entries may repeat.
All inputs are finite; a program needn't handle non-finite values.
Results may differ from a plain program's by a relative error of at most 0.0003.
Values may be sent and summed in bfloat16 or wider, within the bound.
A program may use at most 64 MiB of HBM per device.

v0:
```python
import jax
import jax.numpy as jnp
from jax import lax
from jax.sharding import PartitionSpec as P

PANEL = 128
NB = 256
MOST = 4


broaden = 1.5


def from_everyone(array, axis):
    length = lax.axis_size(axis)
    return lax.all_to_all(
        jnp.broadcast_to(array[None], (length, *array.shape)), axis, 0, 0, tiled=True
    )


def taken_together(array, axis):
    return from_everyone(array, axis).astype(jnp.float32).sum(axis=0)


def sent_together(arrays, axis, split_dim, concat_dim, along):
    both = jnp.concatenate(arrays, axis=along)
    result, at, outs = (
        lax.all_to_all(both, axis, split_axis=split_dim, concat_axis=concat_dim, tiled=True),
        0,
        [],
    )
    for a in arrays:
        outs.append(lax.slice_in_dim(result, at, at + a.shape[along], axis=along))
        at += a.shape[along]
    return tuple(outs)


def kernel_tables():
    freq = lax.broadcasted_iota(jnp.int32, (NB,), 0).astype(jnp.float32) + 0.5
    diff = freq[:, None] - freq[None, :]
    total = freq[:, None] + freq[None, :]
    low = diff * diff + broaden * broaden
    high = total * total + broaden * broaden
    return (diff / low - total / high, broaden / high - broaden / low)


def transform(arrived):
    kernel_re, kernel_im = kernel_tables()
    flat = arrived.reshape(arrived.shape[0], arrived.shape[2])
    real_part = jnp.dot(
        kernel_re, flat, precision=lax.Precision.HIGHEST, preferred_element_type=jnp.float32
    )
    imag_part = jnp.dot(
        kernel_im, flat, precision=lax.Precision.HIGHEST, preferred_element_type=jnp.float32
    )
    return jnp.stack([real_part, imag_part])


def local(pair_density, bin_index, panel_columns):
    trans_count = lax.axis_size("trans")
    bin_place = lax.axis_index("bin")
    local_rows, row_count = pair_density.shape
    per_owner = NB // trans_count
    bin_number = bin_index[:, 0]
    matching = bin_number[:, None] == bin_number[None, :]
    earlier = lax.broadcasted_iota(jnp.int32, (local_rows, local_rows), 0) > lax.broadcasted_iota(
        jnp.int32, (local_rows, local_rows), 1
    )
    rank = jnp.sum((matching & earlier).astype(jnp.int32), axis=1)
    slot = bin_number * MOST + rank
    placing = (lax.broadcasted_iota(jnp.int32, (NB * MOST, local_rows), 0) == slot[None, :]).astype(
        jnp.bfloat16
    )
    selector = (
        lax.broadcasted_iota(jnp.int32, (row_count, PANEL), 0) + bin_place * row_count
        == panel_columns[None, :]
    ).astype(jnp.bfloat16)
    send_rows = jnp.dot(placing, pair_density, preferred_element_type=jnp.float32).astype(
        jnp.bfloat16
    )
    panel = (
        taken_together(
            jnp.dot(pair_density, selector, preferred_element_type=jnp.float32).astype(
                jnp.bfloat16
            ),
            "bin",
        )
        .astype(jnp.float32)
        .astype(jnp.bfloat16)
    )
    send_panel = jnp.dot(placing, panel, preferred_element_type=jnp.float32).astype(jnp.bfloat16)
    got_rows, got_panel = sent_together((send_rows, send_panel), "trans", 0, 0, 1)
    rows_split = got_rows.reshape(trans_count, per_owner, MOST, row_count)
    panel_split = got_panel.reshape(trans_count, per_owner, MOST, PANEL)
    spectral = jnp.einsum(
        "sbmg,sbmc->bgc", rows_split, panel_split, preferred_element_type=jnp.float32
    )
    piece_width = row_count * PANEL // trans_count
    slab = spectral.reshape(per_owner, trans_count, piece_width)
    arrived = lax.all_to_all(slab, "trans", split_axis=1, concat_axis=0, tiled=True)
    response = transform(arrived)
    return response


def solution(mesh):
    placed = (P("trans", "bin"), P("trans", None), P())
    return jax.shard_map(
        local,
        mesh=mesh,
        in_specs=placed,
        out_specs=P(None, None, ("bin", "trans")),
        check_vma=False,
    )
```

profile of v0, /device:TPU:1, one launch (start us, length us, event | category | flops | bytes accessed | tf_op | source)
XLA Modules:
  0.0 201.7 jit_solution(10618374828279506357)
XLA Ops:
  0.0 1.2 copy-done
  1.2 1.3 fusion.9
  2.6 1.1 broadcast_in_dim.2
  3.7 7.7 %all-to-all-start = ((bf16[8,512,128]{2,1,0:T(8,128)(2,1)}), bf16[8,512,128]{2,1,0:T(8,128)(2,1)S(1)}, u32[]{:S(2)}, u32[]{:S(2)}) async-start(bf16[8,512,128]{2,1,0:T(8,128)(2,1)} %broadcast_in_dim.2), calls=%async_computation | async-start | bytes 2097152 | tf_op jit(solution)/shard_map/all_to_all | solution.py:16
  11.4 0.3 convert_reduce_fusion
  11.6 2.6 %fusion.4 = bf16[1024,1000]{0,1:T(8,128)(2,1)} fusion(bf16[512,1000]{0,1:T(8,128)(2,1)S(1)} %copy-done, s32[512]{0:T(512)S(1)} %multiply_add_fusion), kind=kOutput, calls=%fused_computation.9 | convolution fusion | flops 1050124288 | bytes 3074048 | tf_op jit(solution)/shard_map/dot_general | solution.py:78
  14.3 24.3 %all-to-all-done = bf16[8,512,128]{2,1,0:T(8,128)(2,1)S(1)} async-done(((bf16[8,512,128]{2,1,0:T(8,128)(2,1)}), bf16[8,512,128]{2,1,0:T(8,128)(2,1)S(1)}, u32[]{:S(2)}, u32[]{:S(2)}) %all-to-all-start) | async-done | bytes 1048608 | tf_op jit(solution)/shard_map/all_to_all | solution.py:16
  38.6 0.1 reduce_sum.22
  38.7 0.6 fusion.8
  39.3 3.2 %pad_maximum_fusion.1 = bf16[1024,1128]{0,1:T(8,128)(2,1)} fusion(bf16[1024,128]{0,1:T(8,128)(2,1)S(1)} %fusion.8, bf16[1024,1000]{0,1:T(8,128)(2,1)} %fusion.4), kind=kLoop, calls=%fused_computation.3 | loop fusion | flops 4620288 | bytes 4620288 | tf_op jit(solution)/shard_map/concatenate | solution.py:26
  42.5 3.0 %copy.11 = bf16[1024,1128]{1,0:T(8,128)(2,1)S(1)} copy(bf16[1024,1128]{0,1:T(8,128)(2,1)} %pad_maximum_fusion.1) | data formatting | bytes 4620288 | tf_op jit(solution)/shard_map/concatenate | solution.py:26
  45.5 72.6 %all_to_all.32 = bf16[64,16,1128]{2,1,0:T(8,128)(2,1)S(1)} all-to-all(bf16[64,16,1128]{2,1,0:T(8,128)(2,1)S(1)} %bitcast.25), channel_id=1, replica_groups=mesh['trans'=64,'bin'=8] {'trans'}, dimensions={0} | all-to-all | bytes 4620288 | tf_op jit(solution)/shard_map/all_to_all | solution.py:28
  118.2 0.3 slice.8
  118.5 2.2 %reshape.36 = bf16[64,4,4,1000]{3,2,1,0:T(4,128)(2,1)} reshape(bf16[1024,1000]{1,0:T(8,128)(2,1)S(1)} %slice.8) | data formatting | bytes 4096000 | tf_op jit(solution)/shard_map/reshape | solution.py:93
  120.7 5.4 %fusion.5 = f32[4,1000,128]{2,1,0:T(8,128)} fusion(bf16[64,4,4,1000]{3,2,1,0:T(4,128)(2,1)} %reshape.36, bf16[64,4,4,128]{3,2,1,0:T(4,128)(2,1)S(1)} %bitcast.27), kind=kOutput, calls=%fused_computation.10 | convolution fusion | flops 262144000 | bytes 4358144 | tf_op jit(solution)/shard_map/sbmg,sbmc->bgc/dot_general | solution.py:95
  126.1 2.9 %reshape.38 = f32[4,64,2000]{2,1,0:T(8,128)S(1)} reshape(f32[4,1000,128]{2,1,0:T(8,128)} %fusion.5) | data formatting | bytes 4096000 | tf_op jit(solution)/shard_map/reshape | solution.py:99
  129.0 2.7 %copy.14 = f32[4,64,2000]{2,0,1:T(4,128)} copy(f32[4,64,2000]{2,1,0:T(8,128)S(1)} %reshape.38) | data formatting | bytes 4096000 | tf_op jit(solution)/shard_map/reshape | solution.py:99
  131.7 6.0 %all-to-all-start.2 = ((f32[4,64,2000]{2,0,1:T(4,128)}), f32[4,64,2000]{2,0,1:T(4,128)S(1)}, u32[]{:S(2)}, u32[]{:S(2)}) async-start(f32[4,64,2000]{2,0,1:T(4,128)} %copy.14), calls=%async_computation.2 | async-start | bytes 4194304 | tf_op jit(solution)/shard_map/all_to_all | solution.py:100
  137.8 51.2 %all-to-all-done.2 = f32[4,64,2000]{2,0,1:T(4,128)S(1)} async-done(((f32[4,64,2000]{2,0,1:T(4,128)}), f32[4,64,2000]{2,0,1:T(4,128)S(1)}, u32[]{:S(2)}, u32[]{:S(2)}) %all-to-all-start.2) | async-done | bytes 2048032 | tf_op jit(solution)/shard_map/all_to_all | solution.py:100
  189.0 1.3 copy-done.1
  190.3 2.0 reshape.39
  192.3 3.6 %convolution_bitcast_fusion = f32[1,256,2000]{1,2,0:T(8,128)S(1)} fusion(f32[256,2000]{1,0:T(8,128)S(1)} %reshape.39, f32[256]{0:T(256)S(1)} %convert_add_fusion), kind=kOutput, calls=%fused_computation.1 | convolution fusion | flops 1573453824 | bytes 4097024 | tf_op jit(solution)/shard_map/dot_general | solution.py:53
  195.9 3.6 %convolution_bitcast_fusion.1 = f32[1,256,2000]{1,2,0:T(8,128)S(1)} fusion(f32[256,2000]{1,0:T(8,128)S(1)} %reshape.39, f32[256]{0:T(256)S(1)} %convert_add_fusion), kind=kOutput, calls=%fused_computation.2 | convolution fusion | flops 1573453824 | bytes 4097024 | tf_op jit(solution)/shard_map/dot_general | solution.py:50
  199.5 2.2 %pad_maximum_fusion = f32[2,256,2000]{1,2,0:T(8,128)} fusion(f32[1,256,2000]{1,2,0:T(8,128)S(1)} %convolution_bitcast_fusion, f32[1,256,2000]{1,2,0:T(8,128)S(1)} %convolution_bitcast_fusion.1), kind=kLoop, calls=%fused_computation | loop fusion | flops 1024000 | bytes 8192000 | tf_op jit(solution)/shard_map/stack | solution.py:56
  (9 shorter events, 0.3 us)
Async XLA Ops:
  0.0 1.2 copy-start
  1.2 10.2 %copy-start.2 = (s32[512,1]{0,1:T(1,128)S(1)}, s32[512,1]{0,1:T(1,128)}, u32[]{:S(2)}) copy-start(s32[512,1]{0,1:T(1,128)} %param.4) | copy-start | bytes 6148
  3.7 34.8 %all-to-all-start = ((bf16[8,512,128]{2,1,0:T(8,128)(2,1)}), bf16[8,512,128]{2,1,0:T(8,128)(2,1)S(1)}, u32[]{:S(2)}, u32[]{:S(2)}) async-start(bf16[8,512,128]{2,1,0:T(8,128)(2,1)} %broadcast_in_dim.2), calls=%async_computation | async-start | bytes 2097152 | tf_op jit(solution)/shard_map/all_to_all | solution.py:16
  131.7 57.3 %all-to-all-start.2 = ((f32[4,64,2000]{2,0,1:T(4,128)}), f32[4,64,2000]{2,0,1:T(4,128)S(1)}, u32[]{:S(2)}, u32[]{:S(2)}) async-start(f32[4,64,2000]{2,0,1:T(4,128)} %copy.14), calls=%async_computation.2 | async-start | bytes 4194304 | tf_op jit(solution)/shard_map/all_to_all | solution.py:100
  189.0 1.3 copy-start.1
where the time goes:
time: 202 us
  waiting for transfers between devices  75.5 us (37%)
  blocking collectives  72.6 us (36%)
  matrix products  17.1 us (8%)
  local copies, waits for them, and re-layouts  16.9 us (8%)
  starting transfers between devices  13.7 us (7%)
  other arithmetic  5.86 us (3%)
    all_to_all x1, blocking collectives, sent_together(): lax.all_to_all(both, axis, split_axis=split_dim, concat_axis=concat_dim,...  72.6 us
    all_to_all x1, waiting for transfers between devices, local(): lax.all_to_all(slab, 'trans', split_axis=1, concat_axis=0, tiled=True)  51.2 us
    all_to_all x1, waiting for transfers between devices, from_everyone(): lax.all_to_all(jnp.broadcast_to(array[None], (length, *array.shape)), axi...  24.3 us
    all_to_all x1, starting transfers between devices, from_everyone(): lax.all_to_all(jnp.broadcast_to(array[None], (length, *array.shape)), axi...  7.65 us
    all_to_all x1, starting transfers between devices, local(): lax.all_to_all(slab, 'trans', split_axis=1, concat_axis=0, tiled=True)  6.04 us
    reshape x2, local copies, waits for them, and re-layouts, local(): slab = spectral.reshape(per_owner, trans_count, piece_width)  5.58 us
    dot_general x1, matrix products, local(): jnp.einsum('sbmg,sbmc->bgc', rows_split, panel_split, preferred_element_t...  5.39 us
  transfers between devices with their start and end apart: 2, of which 2 were waited for; matrix products, arithmetic and copies ran while one was open for 1% of the time, Pallas kernels for 0%

commit v1 on v0

v1 whole, which is shorter than its diff:
```python
import functools

import jax
import jax.numpy as jnp
from jax import lax
from jax.experimental import pallas as pl
from jax.experimental.pallas import tpu as pltpu
from jax.sharding import PartitionSpec as P

PANEL = 128
NB = 256
BROADEN = 1.5
ZN, XN, YN = 8, 4, 8
NT = 64
QUARTERS = 4
WINDOW = 18
MSG = WINDOW * QUARTERS
HALF = 32
PD_EARLY = 16
MESH = pl.DeviceIdType.MESH
BF16 = jnp.bfloat16
F32 = jnp.float32


def window_pair(owner):
    return jnp.minimum((owner * 125 // 8) // 2, 491)


def exchange_kernel(pd, part, bins, y_out, bin_out, buf_a, buf_b, slots, piece, *sems):
    (pd_s, pd_r, bn_s, bn_r, loc, y0_s, y0_r, za_s, za_r, zb_s, zb_r, xa_s, xa_r, ra_s, ra_r, rb_s, rb_r,
     rx_s, rx_r, ca_s, ca_r, cb_s, cb_r) = sems
    t, y = lax.axis_index("trans"), lax.axis_index("bin")
    core, chip = lax.rem(t, 2), t // 2
    x, z = chip // ZN, lax.rem(chip, ZN)

    barrier = pltpu.get_barrier_semaphore()

    def greet(k, carry):
        pl.semaphore_signal(barrier, inc=1, device_id=(lax.rem(t + k, NT), y), device_id_type=MESH)
        return carry

    def greet_y(k, carry):
        pl.semaphore_signal(barrier, inc=1, device_id=(t, lax.rem(y + k, YN)), device_id_type=MESH)
        return carry

    lax.fori_loop(1, NT, greet, 0)
    lax.fori_loop(1, YN, greet_y, 0)
    pl.semaphore_wait(barrier, NT - 1 + YN - 1)

    def remote(src, dst, send, recv, device):
        return pltpu.make_async_remote_copy(
            src_ref=src, dst_ref=dst, send_sem=send, recv_sem=recv, device_id=device, device_id_type=MESH
        )

    sent = []

    def go(copy):
        copy.start()
        sent.append(copy)
        return copy

    def rows(start, size):
        return pl.ds(pl.multiple_of(start, 8), size)

    for k in range(1, YN):
        to = lax.rem(y + k, YN)
        go(remote(part.at[rows(to * 64, 64)], slots.at[y], y0_s.at[k], y0_r.at[k], (t, to)))
    own = pltpu.make_async_copy(part.at[rows(y * 64, 64)], slots.at[y], loc.at[0])
    own.start()

    def pd_copy(k, to, frm):
        return remote(
            pd.at[rows(window_pair(to) * 8, MSG)], y_out.at[rows(frm * MSG, MSG)], pd_s.at[k], pd_r.at[k], (to, y)
        )

    def bin_copy(k, to, frm):
        return remote(bins, bin_out.at[rows(frm * 8, 8)], bn_s.at[k], bn_r.at[k], (to, y))

    def pd_start(k, carry):
        to = lax.rem(t + k, NT)
        pd_copy(k, to, t).start()
        bin_copy(k, to, t).start()
        return carry

    lax.fori_loop(1, PD_EARLY, pd_start, 0)
    own_pd = pltpu.make_async_copy(pd.at[rows(window_pair(t) * 8, MSG)], y_out.at[rows(t * MSG, MSG)], loc.at[1])
    own_pd.start()
    own_bin = pltpu.make_async_copy(bins, bin_out.at[rows(t * 8, 8)], loc.at[2])
    own_bin.start()

    own.wait()
    for k in range(1, YN):
        frm = lax.rem(y - k + YN, YN)
        remote(part.at[rows(0, 64)], slots.at[frm], y0_s.at[k], y0_r.at[k], (t, frm)).wait_recv()
    total = slots[0].astype(F32)
    for k in range(1, YN):
        total = total + slots[k].astype(F32)
    piece[...] = total.astype(BF16)

    a_own = buf_a.at[core * YN + y, rows(chip * HALF, HALF)]
    b_own = buf_b.at[core * XN + x, rows((y * ZN + z) * HALF, HALF)]
    pa, pb = piece.at[rows(0, HALF)], piece.at[rows(HALF, HALF)]
    la = pltpu.make_async_copy(pa, a_own, loc.at[3])
    lb = pltpu.make_async_copy(pb, b_own, loc.at[4])
    la.start()
    lb.start()
    for k in range(1, ZN):
        to = (x * ZN + lax.rem(z + k, ZN)) * 2 + core
        go(remote(pb, b_own, zb_s.at[k], zb_r.at[k], (to, y)))
        go(remote(pa, a_own, za_s.at[k], za_r.at[k], (to, y)))
    la.wait()
    lb.wait()
    for k in range(1, ZN):
        zf = lax.rem(z - k + ZN, ZN)
        frm = (x * ZN + zf) * 2 + core
        b_dst = buf_b.at[core * XN + x, rows((y * ZN + zf) * HALF, HALF)]
        a_dst = buf_a.at[core * YN + y, rows((x * ZN + zf) * HALF, HALF)]
        remote(pb, b_dst, zb_s.at[k], zb_r.at[k], (frm, y)).wait_recv()
        remote(pa, a_dst, za_s.at[k], za_r.at[k], (frm, y)).wait_recv()

    y_right, y_left = lax.rem(y + 1, YN), lax.rem(y + YN - 1, YN)

    def b_part(yy, half=None):
        base, size = lax.rem(yy + 2 * YN, YN) * (ZN * HALF), ZN * HALF
        if half is not None:
            base, size = base + half * (size // 2), size // 2
        return buf_b.at[core * XN + x, rows(base, size)]

    def a_part(yy, half=None):
        lead = core * YN + lax.rem(yy + 2 * YN, YN)
        if half is None:
            return buf_a.at[lead]
        return buf_a.at[lead, rows(half * 512, 512)]

    def x_part(xx, half=None):
        lead = core * XN + lax.rem(xx + 2 * XN, XN)
        if half is None:
            return buf_b.at[lead]
        return buf_b.at[lead, rows(half * 1024, 1024)]

    def ring_send(part_of, me, s, last, send, recv, right, left):
        h = s == last
        r_ref = part_of(me - s, 0 if h else None)
        l_ref = part_of(me + s, 1 if h else None)
        go(remote(r_ref, r_ref, send.at[0, s], recv.at[0, s], right))
        go(remote(l_ref, l_ref, send.at[1, s], recv.at[1, s], left))

    def ring_wait(part_of, me, s, last, send, recv, right, left):
        h = s == last
        r_ref = part_of(me - 1 - s, 0 if h else None)
        l_ref = part_of(me + 1 + s, 1 if h else None)
        remote(r_ref, r_ref, send.at[0, s], recv.at[0, s], left).wait_recv()
        remote(l_ref, l_ref, send.at[1, s], recv.at[1, s], right).wait_recv()

    ring_b = (b_part, y, rb_s, rb_r, (t, y_right), (t, y_left))
    ring_a = (a_part, y, ra_s, ra_r, (t, y_right), (t, y_left))
    xr = (lax.rem(x + 1, XN) * ZN + z) * 2 + core
    xl = (lax.rem(x + XN - 1, XN) * ZN + z) * 2 + core
    ring_x = (x_part, x, rx_s, rx_r, (xr, y), (xl, y))

    def send(ring, s, last):
        ring_send(ring[0], ring[1], s, last, *ring[2:])

    def wait(ring, s, last):
        ring_wait(ring[0], ring[1], s, last, *ring[2:])

    mate = t + 1 - 2 * core

    def pass_a(r):
        ref = a_part(y + r)
        go(remote(ref, ref, ca_s.at[r % YN], ca_r.at[r % YN], (mate, y)))

    def pass_b(r):
        ref = x_part(x + r)
        go(remote(ref, ref, cb_s.at[r % XN], cb_r.at[r % XN], (mate, y)))

    send(ring_b, 0, 3)
    for k in range(1, XN):
        to = (lax.rem(x + k, XN) * ZN + z) * 2 + core
        ref = buf_a.at[core * YN + y, rows(x * (ZN * HALF), ZN * HALF)]
        go(remote(ref, ref, xa_s.at[k], xa_r.at[k], (to, y)))
    lax.fori_loop(PD_EARLY, NT, pd_start, 0)
    for k in range(1, XN):
        xf = lax.rem(x - k + XN, XN)
        frm = (xf * ZN + z) * 2 + core
        ref = buf_a.at[core * YN + y, rows(xf * (ZN * HALF), ZN * HALF)]
        remote(ref, ref, xa_s.at[k], xa_r.at[k], (frm, y)).wait_recv()
    send(ring_a, 0, 3)
    pass_a(0)
    for s in range(3):
        wait(ring_b, s, 3)
        send(ring_b, s + 1, 3)
    wait(ring_b, 3, 3)
    send(ring_x, 0, 1)
    pass_b(0)
    for s in range(3):
        wait(ring_a, s, 3)
        send(ring_a, s + 1, 3)
        pass_a(-1 - s)
        pass_a(1 + s)
    wait(ring_x, 0, 1)
    send(ring_x, 1, 1)
    pass_b(-1)
    pass_b(1)
    wait(ring_a, 3, 3)
    pass_a(4)
    wait(ring_x, 1, 1)
    pass_b(2)

    own_pd.wait()
    own_bin.wait()

    def pd_wait(k, carry):
        frm = lax.rem(t - k + NT, NT)
        pd_copy(k, frm, frm).wait()
        bin_copy(k, frm, frm).wait()
        return carry

    lax.fori_loop(1, NT, pd_wait, 0)
    for copy in sent:
        copy.wait_send()
    for r in range(YN):
        ref = buf_a.at[(1 - core) * YN + lax.rem(y + r, YN)]
        remote(ref, ref, ca_s.at[r], ca_r.at[r], (mate, y)).wait_recv()
    for r in range(XN):
        ref = buf_b.at[(1 - core) * XN + lax.rem(x + r, XN)]
        remote(ref, ref, cb_s.at[r], cb_r.at[r], (mate, y)).wait_recv()


def exchange(pd, part, bins):
    dma = pltpu.SemaphoreType.DMA
    anyspace = pl.BlockSpec(memory_space=pl.ANY)
    return pl.pallas_call(
        exchange_kernel,
        out_shape=(
            jax.ShapeDtypeStruct((NT * MSG, 128), BF16),
            jax.ShapeDtypeStruct((NT * 8, 128), BF16),
            jax.ShapeDtypeStruct((2 * YN, XN * ZN * HALF, PANEL), BF16),
            jax.ShapeDtypeStruct((2 * XN, YN * ZN * HALF, PANEL), BF16),
        ),
        in_specs=[anyspace] * 3,
        out_specs=(anyspace,) * 4,
        scratch_shapes=[
            pltpu.VMEM((YN, 64, PANEL), BF16),
            pltpu.VMEM((64, PANEL), BF16),
            dma((NT,)), dma((NT,)), dma((NT,)), dma((NT,)), dma((5,)),
            dma((YN,)), dma((YN,)),
            dma((ZN,)), dma((ZN,)), dma((ZN,)), dma((ZN,)),
            dma((XN,)), dma((XN,)),
            dma((2, 4)), dma((2, 4)), dma((2, 4)), dma((2, 4)), dma((2, 2)), dma((2, 2)),
            dma((YN,)), dma((YN,)), dma((XN,)), dma((XN,)),
        ],
        compiler_params=pltpu.CompilerParams(collective_id=1, has_side_effects=True),
        name="exchange",
    )(pd, part, bins)


GROUPS = 8
KC = 16
ROWS = WINDOW * 16


def spectral_kernel(y_ref, bin_ref, a_ref, b_ref, table, o_ref, yf, key, par, lhs, rhs, acc, shi, slo, kh, kl):
    t = lax.axis_index("trans")
    first = 125 * t // 8
    shift = lax.rem(80 * t, 128)
    skip = first - 2 * window_pair(t)

    yf[...] = y_ref[...].astype(F32)
    bins = bin_ref[...].astype(F32)
    group = jnp.floor(bins * (1 / 32))
    inner = bins - group * 32
    parity = jnp.floor(inner * (1 / 16))
    key[...] = group * 16 + (inner - parity * 16)
    par[...] = parity
    acc[...] = jnp.zeros_like(acc)
    line = lax.broadcasted_iota(jnp.int32, (NT * 8, 128), 0) % 8
    low = lax.broadcasted_iota(jnp.int32, (16, 128), 0).astype(F32)

    def quarter(q, carry):
        here = line == q
        g_lo = jnp.min(jnp.where(here, group, 1e3)).astype(jnp.int32)
        g_hi = jnp.max(jnp.where(here, group, -1.0)).astype(jnp.int32)

        def build(chip, c2):
            x, z = chip // ZN, lax.rem(chip, ZN)
            for core in range(2):
                src = chip * 2 + core
                odd = jnp.broadcast_to(par[pl.ds(src * 8 + q, 1), :], (128, 128)).T.astype(BF16)
                pieces = []
                for i in range(2):
                    yy = 2 * q + i
                    pieces.append(a_ref[core * YN + yy, pl.ds(pl.multiple_of(chip * HALF, HALF), HALF), :])
                    pieces.append(
                        b_ref[core * XN + x, pl.ds(pl.multiple_of((yy * ZN + z) * HALF, HALF), HALF), :]
                    )
                block = jnp.concatenate(pieces, axis=0)
                high = block * odd
                at = pl.ds(pl.multiple_of(src * 128, 128), 128)
                rhs[at, 128:256] = high
                rhs[at, 0:128] = block - high
            return c2

        lax.fori_loop(0, NT // 2, build, 0)

        def one_group(g, c2):
            want = low + (g * 16).astype(F32)

            def chunk(k, c3):
                for i in range(KC):
                    src = k * KC + i
                    mask = jnp.broadcast_to(key[pl.ds(src * 8 + q, 1), :], (16, 128)) == want
                    for w in range(WINDOW):
                        row = jnp.broadcast_to(yf[pl.ds(src * MSG + w * QUARTERS + q, 1), :], (16, 128))
                        lhs[w * 16:(w + 1) * 16, i * 128:(i + 1) * 128] = jnp.where(mask, row, 0.0).astype(BF16)
                at = pl.ds(pl.multiple_of(k * (KC * 128), 128), KC * 128)
                acc[g, 0:ROWS, :] += jnp.dot(lhs[...], rhs[at, :], preferred_element_type=F32)
                return c3

            return lax.fori_loop(0, NT // KC, chunk, c2)

        return lax.fori_loop(g_lo, g_hi + 1, one_group, carry)

    lax.fori_loop(0, QUARTERS, quarter, 0)

    lane = lax.broadcasted_iota(jnp.int32, (16, 128), 1)

    def align(k, carry):
        for g in range(GROUPS):
            for p in range(2):
                cols = slice(p * 128, (p + 1) * 128)
                this = acc[g, pl.ds(pl.multiple_of((skip + k) * 16, 16), 16), cols]
                after = acc[g, pl.ds(pl.multiple_of((skip + k + 1) * 16, 16), 16), cols]
                turned = pltpu.roll(jnp.where(lane < shift, after, this), lax.rem(128 - shift, 128), 1)
                hi = turned.astype(BF16)
                at = pl.ds(pl.multiple_of(k * 128, 128), 128)
                r0 = g * 32 + p * 16
                shi[r0:r0 + 16, at] = hi
                slo[r0:r0 + 16, at] = (turned - hi.astype(F32)).astype(BF16)
        return carry

    lax.fori_loop(0, 16, align, 0)
    dot = functools.partial(jnp.dot, preferred_element_type=F32)
    kh[...] = table[...].astype(BF16)
    kl[...] = (table[...] - kh[...].astype(F32)).astype(BF16)
    for n in range(4):
        width = min(512, 2000 - n * 512)
        at = slice(n * 512, n * 512 + 512)
        part = dot(kh[...], shi[:, at]) + dot(kh[...], slo[:, at]) + dot(kl[...], shi[:, at])
        o_ref[:, n * 512:n * 512 + width] = part[:, :width]


def spectral_response(y_in, bins, a, b, table):
    vm = pl.BlockSpec(memory_space=pltpu.VMEM)
    return pl.pallas_call(
        spectral_kernel,
        out_shape=jax.ShapeDtypeStruct((2 * NB, 2000), F32),
        in_specs=[vm] * 5,
        out_specs=vm,
        scratch_shapes=[
            pltpu.VMEM((NT * MSG, 128), F32),
            pltpu.VMEM((NT * 8, 128), F32),
            pltpu.VMEM((NT * 8, 128), F32),
            pltpu.VMEM((ROWS, KC * 128), BF16),
            pltpu.VMEM((NT * 128, 256), BF16),
            pltpu.VMEM((GROUPS, ROWS + 16, 256), F32),
            pltpu.VMEM((NB, 2048), BF16),
            pltpu.VMEM((NB, 2048), BF16),
            pltpu.VMEM((2 * NB, NB), BF16),
            pltpu.VMEM((2 * NB, NB), BF16),
        ],
        compiler_params=pltpu.CompilerParams(vmem_limit_bytes=60 << 20),
        name="spectral",
    )(y_in, bins, a, b, table)


def kernel_table():
    freq = lax.broadcasted_iota(jnp.int32, (NB, 1), 0).astype(F32) + 0.5
    diff = freq - freq[:, 0][None, :]
    total = freq + freq[:, 0][None, :]
    low = diff * diff + BROADEN * BROADEN
    high = total * total + BROADEN * BROADEN
    return jnp.concatenate([diff / low - total / high, BROADEN / high - BROADEN / low], axis=0)


def local(pair_density, bin_index, panel_columns):
    count, width = pair_density.shape
    place = lax.axis_index("bin")
    bin_number = bin_index[:, 0]
    key = bin_number * count + lax.iota(jnp.int32, count)
    position = jnp.sum((key[None, :] < key[:, None]).astype(jnp.int32), axis=1)
    sorting = lax.broadcasted_iota(jnp.int32, (count, count), 0) == position[None, :]
    perm = sorting.astype(BF16)
    ordered = jnp.sum(jnp.where(sorting, bin_number[None, :], 0), axis=1)
    bins = jnp.pad(ordered.astype(BF16).reshape(QUARTERS, 128), ((0, 4), (0, 0)))
    selector = (
        lax.broadcasted_iota(jnp.int32, (width, PANEL), 0) + place * width == panel_columns[None, :]
    ).astype(BF16)
    turned = lax.dot_general(
        pair_density, perm, (((0,), (1,)), ((), ())), preferred_element_type=F32
    ).astype(BF16)
    part = jnp.dot(pair_density, selector, preferred_element_type=F32).astype(BF16)
    part = jnp.dot(perm, part, preferred_element_type=F32).astype(BF16)
    y_in, all_bins, a, b = exchange(turned.reshape(width * QUARTERS, 128), part, bins)
    return spectral_response(y_in, all_bins, a, b, kernel_table()).reshape(2, NB, 2000)


def solution(mesh):
    placed = (P("trans", "bin"), P("trans", None), P())
    return jax.shard_map(
        local,
        mesh=mesh,
        in_specs=placed,
        out_specs=P(None, None, ("bin", "trans")),
        check_vma=False,
    )
```

time: 202 us -> 151 us (0.75)
  Pallas kernels: 0 us -> 136 us
  waiting for transfers between devices: 75.5 us -> 0 us
  blocking collectives: 72.6 us -> 0 us
  matrix products: 17.1 us -> 2.9 us
  starting transfers between devices: 13.7 us -> 0 us
  local copies, waits for them, and re-layouts: 16.9 us -> 7.45 us
  other arithmetic: 5.86 us -> 3.61 us
    pallas_call x0 -> x2, Pallas kernels: none -> 136 us  [the longest x1 85.7 us: exchange(): pl.pallas_call(exchange_kernel, out_shape=(jax.ShapeDtypeStruct((NT * MSG...]
    all_to_all x2 -> x0, waiting for transfers between devices: 75.5 us -> none  [the longest x1 51.2 us: local(): lax.all_to_all(slab, 'trans', split_axis=1, concat_axis=0, tiled=True)]
    all_to_all x1 -> x0, blocking collectives: 72.6 us -> none  [sent_together(): lax.all_to_all(both, axis, split_axis=split_dim, concat_axis=concat_dim,...]
    dot_general x6 -> x2, matrix products: 17.1 us -> 2.9 us  [the longest x1 2.14 us: local(): part = jnp.dot(perm, part, preferred_element_type=F32).astype(BF16)]
    all_to_all x2 -> x0, starting transfers between devices: 13.7 us -> none  [the longest x1 7.65 us: from_everyone(): lax.all_to_all(jnp.broadcast_to(array[None], (length, *array.shape)), axi...]
    concatenate x1 -> x0, local copies, waits for them, and re-layouts: 2.99 us -> none  [sent_together(): both = jnp.concatenate(arrays, axis=along)]
    reshape x4 -> x2, local copies, waits for them, and re-layouts: 9.75 us -> 6.87 us  [the longest x1 5.3 us: local(): spectral_response(y_in, all_bins, a, b, kernel_table()).reshape(2, NB, 2000)]
    unnamed x6 -> x2, local copies, waits for them, and re-layouts: 2.53 us -> 0.01 us
  transfers between devices with their start and end apart: 2 -> 0, of which waited for: 2 -> 0; matrix products, arithmetic and copies ran while one was open for 1% -> 0% of each run, Pallas kernels for 0% -> 0%
where the time goes in v1:
time: 151 us; the launch traced here: 150 us
  Pallas kernels  136 us (90%)
  local copies, waits for them, and re-layouts  7.45 us (5%)
  other arithmetic  3.61 us (2%)
  matrix products  2.9 us (2%)
    pallas_call x1, Pallas kernels, exchange(): pl.pallas_call(exchange_kernel, out_shape=(jax.ShapeDtypeStruct((NT * MSG...  85.7 us
    pallas_call x1, Pallas kernels, spectral_response(): pl.pallas_call(spectral_kernel, out_shape=jax.ShapeDtypeStruct((2 * NB, 2...  50.7 us
    reshape x1, local copies, waits for them, and re-layouts, local(): spectral_response(y_in, all_bins, a, b, kernel_table()).reshape(2, NB, 2000)  5.3 us

profile of v1, /device:TPU:1, one launch (start us, length us, event | category | flops | bytes accessed | tf_op | source)
XLA Modules:
  0.0 150.4 jit_solution(8594327804637258727)
XLA Ops:
  0.0 0.0 copy-start
  0.0 0.8 iota_add_fusion.2
  0.8 0.7 iota_add_fusion.1
  1.5 0.2 convert_reduce_fusion
  1.7 0.9 select_reduce_fusion
  2.6 0.6 pad.4.bins
  3.2 0.0 copy-done
  3.2 2.1 %convolution_convert_fusion.1.part = bf16[512,128]{1,0:T(8,128)(2,1)} fusion(bf16[512,1000]{0,1:T(8,128)(2,1)S(1)} %copy-done, s32[512]{0:T(512)S(1)} %convert_reduce_fusion, s32[128]{0:T(128)} %param.5, s32[1000]{0:T(1024)S(1)} %iota_add_fusion), kind=kOutput, calls=%fused_computation.2 | convolution fusion | flops 198702080 | bytes 1161632 | tf_op jit(solution)/shard_map/dot_general | solution.py:403
  5.3 0.2 fusion.7
  5.5 0.8 pad_maximum_fusion.table
  6.4 0.8 fusion
  7.1 1.6 %reshape.34.pd = bf16[4000,128]{1,0:T(8,128)(2,1)} reshape(bf16[1000,512]{1,0:T(8,128)(2,1)S(1)} %fusion) | data formatting | bytes 2048000 | tf_op jit(solution)/shard_map/reshape | solution.py:404
  8.7 85.7 %exchange.1 = (bf16[4608,128]{1,0:T(8,128)(2,1)}, bf16[512,128]{1,0:T(8,128)(2,1)}, bf16[16,1024,128]{2,1,0:T(8,128)(2,1)}, bf16[8,2048,128]{2,1,0:T(8,128)(2,1)}) custom-call(bf16[4000,128]{1,0:T(8,128)(2,1)} %reshape.34.pd, bf16[512,128]{1,0:T(8,128)(2,1)} %convolution_convert_fusion.1.part, bf16[8,128]{1,0:T(8,128)(2,1)} %pad.4.bins), custom_call_target="tpu_custom_call" | custom-call | tf_op jit(solution)/shard_map/exchange/pallas_call | solution.py:233
  94.4 50.7 %spectral.1 = f32[512,2000]{1,0:T(8,128)} custom-call(bf16[4608,128]{1,0:T(8,128)(2,1)} %get-tuple-element.9.y_ref, bf16[512,128]{1,0:T(8,128)(2,1)} %get-tuple-element.10.bin_ref, bf16[16,1024,128]{2,1,0:T(8,128)(2,1)} %get-tuple-element.11.a_ref, bf16[8,2048,128]{2,1,0:T(8,128)(2,1)} %get-tuple-element.12.b_ref, f32[512,256]{1,0:T(8,128)} %pad_maximum_fusion.table), custom_call_target="tpu_custom_call" | custom-call | tf_op jit(solution)/shard_map/spectral/pallas_call | solution.py:355
  145.1 5.3 %copy.5 = f32[2,256,2000]{1,2,0:T(8,128)} copy(f32[2,256,2000]{2,1,0:T(8,128)} %bitcast.9) | data formatting | bytes 8192000 | tf_op jit(solution)/shard_map/reshape | solution.py:405
  (3 shorter events, 0.0 us)
Async XLA Ops:
  0.0 3.2 %copy-start = (bf16[512,1000]{0,1:T(8,128)(2,1)S(1)}, bf16[512,1000]{0,1:T(8,128)(2,1)}, u32[]{:S(2)}) copy-start(bf16[512,1000]{0,1:T(8,128)(2,1)} %param.3) | copy-start | bytes 3072004
